TPU v7x, 32 devices: a whole 2x2x4 slice. The times are simulated.
32 devices in a mesh: groups: 2 (over y), inst: 4 (over z), space: 4 (over x, core).
Axes of the slice: x: 2, y: 2, z: 4, core: 2. Of those that a mesh axis runs over, the one named last changes fastest.
Arguments:
- flow_state: float32 [8, 5, 16, 16, 128], P(('groups', 'inst'), None, 'space'), parts along dimension 0, may hold values from -1 to 1
- period_match: int32 [16], replicated, may hold values from 0 to 15, each once
Outputs:
- residual: float32 [8, 5, 16, 16, 128], P(('groups', 'inst'), None, 'space'), parts along dimension 0
There are 2 independent parts, one for each index of `groups`. A program takes and returns all parts, laid end to end along the dimension named above; an argument that names none is the same for every part. Nothing has to cross between parts.
Inputs may be any that keep to these rules, and one draw needn't show every extreme that they name: period_match is a permutation of the 16 spanwise layers.
All inputs are finite; a program needn't handle non-finite values.
Results may differ from a plain program's by a relative error of at most 0.0003.
Values sent between devices are 32-bit elements; how exact they have to be, the bound alone decides.
No kernel may reach another device: no remote copies, remote signals or barrier semaphores. Data moves between devices by JAX's collectives and lax.ppermute only.
A program may use at most 64 MiB of HBM per device.

v0:
```python
import math
import jax
import jax.numpy as jnp
from jax import lax
from jax.sharding import PartitionSpec as P

gamma_gas = 1.4
prandtl = 0.72
viscosity = 0.1
pseudo_step = 0.03
entropy_share = 0.1


def from_behind(block, axis, distance):
    devices = range(lax.axis_size(axis))
    route = [((i - distance) % len(devices), i) for i in devices]
    return lax.ppermute(block, axis, route)


def extended(cells, sides, width):
    for axis, dim in sides:
        count = lax.axis_size(axis)
        ends = count - 1
        head = lax.slice_in_dim(cells, 0, width, axis=dim)
        tail = lax.slice_in_dim(cells, cells.shape[dim] - width, cells.shape[dim], axis=dim)
        cells = jnp.concatenate(
            [
                lax.ppermute(tail, axis, [(i, (i + 1) % count) for i in range(ends)]),
                cells,
                lax.ppermute(head, axis, [((i + 1) % count, i) for i in range(ends)]),
            ],
            axis=dim,
        )
    return cells


def from_draw(draws):
    shape = (5,) + (1,) * (draws.ndim - 1)
    offsets = jnp.array([1.0, 0.8, 0.0, 0.0, 0.8], jnp.float32).reshape(shape)
    spreads = jnp.array([0.3, 0.3, 0.3, 0.3, 0.2], jnp.float32).reshape(shape)
    return offsets + spreads * draws


def conserved(primitives):
    dens = primitives[0]
    velocity = primitives[1:4]
    kinetic = 0.5 * dens * jnp.sum(velocity * velocity, axis=0)
    energy = primitives[4] / (gamma_gas - 1.0) + kinetic
    return jnp.concatenate([dens[None], dens[None] * velocity, energy[None]], axis=0)


def primitive(conserved_vars):
    dens = conserved_vars[0]
    velocity = conserved_vars[1:4] / dens
    pressure = (gamma_gas - 1.0) * (
        conserved_vars[4] - 0.5 * dens * jnp.sum(velocity * velocity, axis=0)
    )
    return jnp.concatenate([dens[None], velocity, pressure[None]], axis=0)


def entropy_fix(eigen_val, sound_speed):
    spread = entropy_share * sound_speed
    magnitude = jnp.abs(eigen_val)
    return jnp.where(
        magnitude >= spread, magnitude, (eigen_val * eigen_val + spread * spread) / (2.0 * spread)
    )


def euler_flux(dens, velocity, pressure, enthalpy, normal):
    normal_vel = velocity[normal]
    values = [dens * normal_vel]
    for component in range(3):
        moment = dens * velocity[component] * normal_vel
        if component == normal:
            moment = moment + pressure
        values.append(moment)
    values.append(dens * enthalpy * normal_vel)
    return values


def face_flux(left_cells, right_cells, normal):
    dens_left, vel_left, pres_left = (left_cells[0], left_cells[1:4], left_cells[4])
    dens_right, vel_right, pres_right = (right_cells[0], right_cells[1:4], right_cells[4])
    ratio = gamma_gas / (gamma_gas - 1.0)
    sq_left = jnp.sum(vel_left * vel_left, axis=0)
    sq_right = jnp.sum(vel_right * vel_right, axis=0)
    enth_left = ratio * pres_left / dens_left + 0.5 * sq_left
    enth_right = ratio * pres_right / dens_right + 0.5 * sq_right
    flux_left = euler_flux(dens_left, vel_left, pres_left, enth_left, normal)
    flux_right = euler_flux(dens_right, vel_right, pres_right, enth_right, normal)
    root_left = jnp.sqrt(dens_left)
    root_right = jnp.sqrt(dens_right)
    root_sum = root_left + root_right
    vel_roe = (root_left * vel_left + root_right * vel_right) / root_sum
    enth_roe = (root_left * enth_left + root_right * enth_right) / root_sum
    speed_sq = jnp.sum(vel_roe * vel_roe, axis=0)
    sound_sq = (gamma_gas - 1.0) * (enth_roe - 0.5 * speed_sq)
    sound_speed = jnp.sqrt(sound_sq)
    normal_vel = vel_roe[normal]
    dens_roe = root_left * root_right
    jump_dens = dens_right - dens_left
    jump_pres = pres_right - pres_left
    jump_vel = vel_right - vel_left
    jump_normal = jump_vel[normal]
    wave_slow = (jump_pres - dens_roe * sound_speed * jump_normal) / (2.0 * sound_sq)
    wave_fast = (jump_pres + dens_roe * sound_speed * jump_normal) / (2.0 * sound_sq)
    wave_mid = jump_dens - jump_pres / sound_sq
    eigen_mid = entropy_fix(normal_vel, sound_speed)
    flux_slow = entropy_fix(normal_vel - sound_speed, sound_speed) * wave_slow
    flux_fast = entropy_fix(normal_vel + sound_speed, sound_speed) * wave_fast
    dissipation = [flux_slow + eigen_mid * wave_mid + flux_fast]
    for component in range(3):
        unit_dir = 1.0 if component == normal else 0.0
        term = flux_slow * (vel_roe[component] - unit_dir * sound_speed)
        term = term + eigen_mid * (
            wave_mid * vel_roe[component]
            + dens_roe * (jump_vel[component] - unit_dir * jump_normal)
        )
        term = term + flux_fast * (vel_roe[component] + unit_dir * sound_speed)
        dissipation.append(term)
    shear_work = jnp.sum(vel_roe * jump_vel, axis=0) - normal_vel * jump_normal
    energy_term = flux_slow * (enth_roe - normal_vel * sound_speed)
    energy_term = energy_term + eigen_mid * (wave_mid * 0.5 * speed_sq + dens_roe * shear_work)
    energy_term = energy_term + flux_fast * (enth_roe + normal_vel * sound_speed)
    dissipation.append(energy_term)
    jump_temp = pres_right / dens_right - pres_left / dens_left
    jump_kin = 0.5 * (sq_right - sq_left)
    viscous_terms = [
        jnp.zeros_like(jump_dens),
        jump_vel[0],
        jump_vel[1],
        jump_vel[2],
        jump_kin + gamma_gas / ((gamma_gas - 1.0) * prandtl) * jump_temp,
    ]
    values = []
    for component in range(5):
        values.append(
            0.5 * (flux_left[component] + flux_right[component])
            - 0.5 * dissipation[component]
            - viscosity * viscous_terms[component]
        )
    return jnp.stack(values, axis=0)


def flux_change(padded, along, normal):
    length = padded.shape[along]
    face_values = face_flux(
        lax.slice_in_dim(padded, 0, length - 1, axis=along),
        lax.slice_in_dim(padded, 1, length, axis=along),
        normal,
    )
    return lax.slice_in_dim(face_values, 1, length - 1, axis=along) - lax.slice_in_dim(
        face_values, 0, length - 2, axis=along
    )


def spectral_entry(offset, number):
    wrapped = jnp.mod(offset, number)
    parity = 1.0 - 2.0 * jnp.mod(wrapped, 2).astype(jnp.float32)
    angles = math.pi * wrapped.astype(jnp.float32) / number
    sine_val = jnp.where(wrapped == 0, 1.0, jnp.sin(angles))
    derivative = jnp.where(
        wrapped == 0, 0.0, math.pi / number * parity * jnp.cos(angles) / sine_val
    )
    return derivative + 0.5 * parity


def on_device(flow_state, period_match):
    instances = lax.axis_size("inst")
    phase_lag = instances // 4
    instance = lax.axis_index("inst")
    space_parts = lax.axis_size("space")
    position = lax.axis_index("space")
    labels = jnp.arange(period_match.shape[0], dtype=jnp.int32)
    matches = (period_match[:, None] == labels[None, :]).astype(jnp.int32)
    inverse = jnp.sum(labels[:, None] * matches, axis=0)
    mirror = jnp.array([1.0, 1.0, 1.0, -1.0, 1.0], jnp.float32).reshape(5, 1, 1, 1)

    def lagged(plane, steps):
        return from_behind(plane, "inst", steps)

    def timewise(conserved_vars):
        pieces = lax.all_gather(conserved_vars[None], "inst", axis=0, tiled=True)
        number = pieces.shape[0]
        others = jnp.arange(number, dtype=jnp.int32)
        weights = spectral_entry(instance - others, instances)
        return jnp.tensordot(weights, pieces, axes=1, precision=lax.Precision.HIGHEST)

    def evaluate(conserved_vars):
        prims = primitive(conserved_vars)
        padded = extended(prims, (("space", 1),), 1)
        lower_edge = jnp.where(position == 0, prims[:, :1], padded[:, :1])
        upper_edge = jnp.where(position == space_parts - 1, prims[:, -1:], padded[:, -1:])
        along_axial = jnp.concatenate([lower_edge, prims, upper_edge], axis=1)
        along_span = jnp.concatenate(
            [prims[:, :, :1] * mirror, prims, prims[:, :, -1:] * mirror], axis=2
        )
        ghost_below = jnp.take(lagged(prims[..., -1], phase_lag), period_match, axis=2)
        ghost_above = jnp.take(lagged(prims[..., 0], -phase_lag), inverse, axis=2)
        along_pitch = jnp.concatenate(
            [ghost_below[..., None], prims, ghost_above[..., None]], axis=3
        )
        spatial = (
            flux_change(along_axial, 1, 0)
            + flux_change(along_span, 2, 2)
            + flux_change(along_pitch, 3, 1)
        )
        return timewise(conserved_vars) + spatial

    initial = conserved(from_draw(flow_state[0]))
    section_state = initial - pseudo_step * evaluate(initial)
    return evaluate(section_state)[None]


def solution(mesh):
    in_specs = (P(("groups", "inst"), None, "space", None, None), P())
    out_specs = P(("groups", "inst"), None, "space", None, None)
    return jax.shard_map(
        on_device, mesh=mesh, in_specs=in_specs, out_specs=out_specs, check_vma=False
    )
```

profile of v0, /device:TPU:1, one launch (start us, length us, event | category | flops | bytes accessed | tf_op | source)
XLA Modules:
  0.0 72.5 jit_solution(7410314620236597218)
XLA Ops:
  0.0 0.7 copy-done.1
  0.7 1.0 %fusion.15 = f32[5,4,16,128]{3,2,1,0:T(8,128)S(1)} fusion(f32[1,5,4,16,128]{4,3,2,1,0:T(8,128)} %param.7, f32[5]{0:T(128)S(1)} %copy-done.1, f32[5]{0:T(128)S(1)} %copy-done.2), kind=kLoop, calls=%fused_computation.59 | loop fusion | flops 81920 | bytes 327720 | tf_op jit(solution)/shard_map/add | solution.py:41
  1.9 0.5 copy.46
  2.4 2.2 %collective-permute-start.2 = (f32[5,4,16]{0,1,2:T(4,128)S(1)}, f32[5,4,16]{0,1,2:T(4,128)S(1)}, u32[]{:S(2)}, u32[]{:S(2)}) collective-permute-start(f32[5,4,16]{0,1,2:T(4,128)S(1)} %bitcast.389), channel_id=1, source_target_pairs={{12,0},{0,4},{4,8},{8,12},{13,1},{1,5},{5,9},{9,13},{14,2},{2,6},{... | collective-permute-start | bytes 3848 | tf_op jit(solution)/shard_map/ppermute | solution.py:17
  5.0 2.1 %collective-permute-start.3 = (f32[5,4,16]{0,1,2:T(4,128)S(1)}, f32[5,4,16]{0,1,2:T(4,128)S(1)}, u32[]{:S(2)}, u32[]{:S(2)}) collective-permute-start(f32[5,4,16]{0,1,2:T(4,128)S(1)} %bitcast.388), channel_id=1, source_target_pairs={{4,0},{8,4},{12,8},{0,12},{5,1},{9,5},{13,9},{1,13},{6,2},{10,6},{... | collective-permute-start | bytes 3848 | tf_op jit(solution)/shard_map/ppermute | solution.py:17
  7.1 4.2 %collective-permute-start = (f32[5,1,16,128]{3,2,1,0:T(8,128)S(1)}, f32[5,1,16,128]{3,2,1,0:T(8,128)S(1)}, u32[]{:S(2)}, u32[]{:S(2)}) collective-permute-start(f32[5,1,16,128]{3,2,1,0:T(8,128)S(1)} %get-tuple-element.119), channel_id=1, source_target_pairs={{0,1},{1,2},{2,3},{4,5},{5,6},{6,7},{8,9},{9,10},{10,11},{12,13},{... | collective-permute-start | bytes 122888 | tf_op jit(solution)/shard_map/ppermute | solution.py:28
  11.3 1.9 %collective-permute-start.1 = (f32[5,1,16,128]{3,2,1,0:T(8,128)S(1)}, f32[5,1,16,128]{3,2,1,0:T(8,128)S(1)}, u32[]{:S(2)}, u32[]{:S(2)}) collective-permute-start(f32[5,1,16,128]{3,2,1,0:T(8,128)S(1)} %get-tuple-element.120), channel_id=1, source_target_pairs={{1,0},{2,1},{3,2},{5,4},{6,5},{7,6},{9,8},{10,9},{11,10},{13,12},{... | collective-permute-start | bytes 122888 | tf_op jit(solution)/shard_map/ppermute | solution.py:30
  13.4 13.8 %all-gather = f32[20,4,16,128]{3,2,1,0:T(8,128)S(1)} all-gather(f32[5,4,16,128]{3,2,1,0:T(8,128)S(1)} %get-tuple-element.130), channel_id=2, replica_groups=mesh['groups'=2,'inst'=4,'space'=4] {'inst'}, dimensions={0}, use_global_device_ids=true | all-gather | bytes 819200 | tf_op jit(solution)/shard_map/all_gather | solution.py:183
  27.2 0.6 copy-done
  28.6 1.5 %fusion.2 = f32[1,5,4,16,128]{4,0,3,2,1:T(1,128)S(1)} fusion(f32[4,5,4,16,128]{4,3,2,1,0:T(8,128)S(1)} %bitcast.384, s32[]{:T(128)S(6)} %axis_index.23), kind=kOutput, calls=%fused_computation.6 | convolution fusion | flops 1966224 | bytes 819204 | tf_op jit(solution)/shard_map/dot_general | solution.py:187
  30.3 0.6 gather_fusion
  31.0 0.6 copy.31
  31.6 0.6 gather_fusion.1
  32.3 0.6 copy.34
  34.9 14.5 %all-gather.1 = f32[20,4,16,128]{3,2,1,0:T(8,128)S(1)} all-gather(f32[5,4,16,128]{3,2,1,0:T(8,128)S(1)} %fusion.13), channel_id=3, replica_groups=mesh['groups'=2,'inst'=4,'space'=4] {'inst'}, dimensions={0}, use_global_device_ids=true | all-gather | bytes 819200 | tf_op jit(solution)/shard_map/all_gather | solution.py:183
  49.6 1.5 %fusion = f32[1,5,4,16,128]{4,0,3,2,1:T(1,128)S(1)} fusion(f32[4,5,4,16,128]{4,3,2,1,0:T(8,128)S(1)} %bitcast.385, s32[]{:T(128)S(6)} %axis_index.23), kind=kOutput, calls=%fused_computation.4 | convolution fusion | flops 1966224 | bytes 819204 | tf_op jit(solution)/shard_map/dot_general | solution.py:187
  52.2 3.3 %collective-permute-start.7 = (f32[5,4,16]{0,1,2:T(4,128)S(1)}, f32[5,4,16]{0,1,2:T(4,128)S(1)}, u32[]{:S(2)}, u32[]{:S(2)}) collective-permute-start(f32[5,4,16]{0,1,2:T(4,128)S(1)} %bitcast.390), channel_id=1, source_target_pairs={{4,0},{8,4},{12,8},{0,12},{5,1},{9,5},{13,9},{1,13},{6,2},{10,6},{... | collective-permute-start | bytes 3848 | tf_op jit(solution)/shard_map/ppermute | solution.py:17
  56.1 8.9 %collective-permute-start.4 = (f32[5,1,16,128]{3,2,1,0:T(8,128)S(1)}, f32[5,1,16,128]{3,2,1,0:T(8,128)S(1)}, u32[]{:S(2)}, u32[]{:S(2)}) collective-permute-start(f32[5,1,16,128]{3,2,1,0:T(8,128)S(1)} %get-tuple-element.105), channel_id=1, source_target_pairs={{0,1},{1,2},{2,3},{4,5},{5,6},{6,7},{8,9},{9,10},{10,11},{12,13},{... | collective-permute-start | bytes 122888 | tf_op jit(solution)/shard_map/ppermute | solution.py:28
  65.0 2.1 %collective-permute-start.5 = (f32[5,1,16,128]{3,2,1,0:T(8,128)S(1)}, f32[5,1,16,128]{3,2,1,0:T(8,128)S(1)}, u32[]{:S(2)}, u32[]{:S(2)}) collective-permute-start(f32[5,1,16,128]{3,2,1,0:T(8,128)S(1)} %get-tuple-element.106), channel_id=1, source_target_pairs={{1,0},{2,1},{3,2},{5,4},{6,5},{7,6},{9,8},{10,9},{11,10},{13,12},{... | collective-permute-start | bytes 122888 | tf_op jit(solution)/shard_map/ppermute | solution.py:30
  67.3 0.6 gather_fusion.2
  68.0 0.6 copy.36
  68.5 0.6 gather_fusion.3
  69.2 0.6 copy.39
  71.7 0.8 %fusion.8 = f32[1,5,4,16,128]{4,3,2,1,0:T(8,128)} fusion(f32[5,4,16,128]{3,2,1,0:T(8,128)S(1)} %bitcast.386, f32[5,4,16,129]{3,2,1,0:T(8,128)S(1)} %fusion.50, f32[5,4,17,128]{3,2,1,0:T(8,128)S(1)} %constant_dynamic-update-slice_fusion.15, f32[5,5,16,128]{3,2,1,0:T(8,128)S(1)} %constant_dynamic-update-slice_fusion.10), kind=kLoop, calls=%fused_computation.45 | loop fusion | flops 245760 | bytes 1310720 | tf_op jit(solution)/shard_map/broadcast_in_dim | solution.py:212
  (94 shorter events, 7.8 us)
Async XLA Ops:
  0.0 0.7 copy-start.1
  0.0 0.7 copy-start.2
  2.4 27.9 %collective-permute-start.2 = (f32[5,4,16]{0,1,2:T(4,128)S(1)}, f32[5,4,16]{0,1,2:T(4,128)S(1)}, u32[]{:S(2)}, u32[]{:S(2)}) collective-permute-start(f32[5,4,16]{0,1,2:T(4,128)S(1)} %bitcast.389), channel_id=1, source_target_pairs={{12,0},{0,4},{4,8},{8,12},{13,1},{1,5},{5,9},{9,13},{14,2},{2,6},{... | collective-permute-start | bytes 3848 | tf_op jit(solution)/shard_map/ppermute | solution.py:17
  5.0 26.5 %collective-permute-start.3 = (f32[5,4,16]{0,1,2:T(4,128)S(1)}, f32[5,4,16]{0,1,2:T(4,128)S(1)}, u32[]{:S(2)}, u32[]{:S(2)}) collective-permute-start(f32[5,4,16]{0,1,2:T(4,128)S(1)} %bitcast.388), channel_id=1, source_target_pairs={{4,0},{8,4},{12,8},{0,12},{5,1},{9,5},{13,9},{1,13},{6,2},{10,6},{... | collective-permute-start | bytes 3848 | tf_op jit(solution)/shard_map/ppermute | solution.py:17
  7.1 26.9 %collective-permute-start = (f32[5,1,16,128]{3,2,1,0:T(8,128)S(1)}, f32[5,1,16,128]{3,2,1,0:T(8,128)S(1)}, u32[]{:S(2)}, u32[]{:S(2)}) collective-permute-start(f32[5,1,16,128]{3,2,1,0:T(8,128)S(1)} %get-tuple-element.119), channel_id=1, source_target_pairs={{0,1},{1,2},{2,3},{4,5},{5,6},{6,7},{8,9},{9,10},{10,11},{12,13},{... | collective-permute-start | bytes 122888 | tf_op jit(solution)/shard_map/ppermute | solution.py:28
  11.3 1.9 %copy-start.3 = (s32[16]{0:T(128)S(1)}, s32[16]{0:T(128)}, u32[]{:S(2)}) copy-start(s32[16]{0:T(128)} %param.8) | copy-start | bytes 196
  11.3 22.7 %collective-permute-start.1 = (f32[5,1,16,128]{3,2,1,0:T(8,128)S(1)}, f32[5,1,16,128]{3,2,1,0:T(8,128)S(1)}, u32[]{:S(2)}, u32[]{:S(2)}) collective-permute-start(f32[5,1,16,128]{3,2,1,0:T(8,128)S(1)} %get-tuple-element.120), channel_id=1, source_target_pairs={{1,0},{2,1},{3,2},{5,4},{6,5},{7,6},{9,8},{10,9},{11,10},{13,12},{... | collective-permute-start | bytes 122888 | tf_op jit(solution)/shard_map/ppermute | solution.py:30
  27.2 0.7 copy-start
  51.7 15.6 %collective-permute-start.6 = (f32[5,4,16]{0,1,2:T(4,128)S(1)}, f32[5,4,16]{0,1,2:T(4,128)S(1)}, u32[]{:S(2)}, u32[]{:S(2)}) collective-permute-start(f32[5,4,16]{0,1,2:T(4,128)S(1)} %bitcast.391), channel_id=1, source_target_pairs={{12,0},{0,4},{4,8},{8,12},{13,1},{1,5},{5,9},{9,13},{14,2},{2,6},{... | collective-permute-start | bytes 3848 | tf_op jit(solution)/shard_map/ppermute | solution.py:17
  52.2 16.3 %collective-permute-start.7 = (f32[5,4,16]{0,1,2:T(4,128)S(1)}, f32[5,4,16]{0,1,2:T(4,128)S(1)}, u32[]{:S(2)}, u32[]{:S(2)}) collective-permute-start(f32[5,4,16]{0,1,2:T(4,128)S(1)} %bitcast.390), channel_id=1, source_target_pairs={{4,0},{8,4},{12,8},{0,12},{5,1},{9,5},{13,9},{1,13},{6,2},{10,6},{... | collective-permute-start | bytes 3848 | tf_op jit(solution)/shard_map/ppermute | solution.py:17
  56.1 14.8 %collective-permute-start.4 = (f32[5,1,16,128]{3,2,1,0:T(8,128)S(1)}, f32[5,1,16,128]{3,2,1,0:T(8,128)S(1)}, u32[]{:S(2)}, u32[]{:S(2)}) collective-permute-start(f32[5,1,16,128]{3,2,1,0:T(8,128)S(1)} %get-tuple-element.105), channel_id=1, source_target_pairs={{0,1},{1,2},{2,3},{4,5},{5,6},{6,7},{8,9},{9,10},{10,11},{12,13},{... | collective-permute-start | bytes 122888 | tf_op jit(solution)/shard_map/ppermute | solution.py:28
  65.0 5.9 %collective-permute-start.5 = (f32[5,1,16,128]{3,2,1,0:T(8,128)S(1)}, f32[5,1,16,128]{3,2,1,0:T(8,128)S(1)}, u32[]{:S(2)}, u32[]{:S(2)}) collective-permute-start(f32[5,1,16,128]{3,2,1,0:T(8,128)S(1)} %get-tuple-element.106), channel_id=1, source_target_pairs={{1,0},{2,1},{3,2},{5,4},{6,5},{7,6},{9,8},{10,9},{11,10},{13,12},{... | collective-permute-start | bytes 122888 | tf_op jit(solution)/shard_map/ppermute | solution.py:30
where the time goes:
time: 72.7 us; the launch traced here: 72.5 us
  blocking collectives  28.3 us (39%)
  starting transfers between devices  24.6 us (34%)
  local copies, waits for them, and re-layouts  8.14 us (11%)
  other arithmetic  7.8 us (11%)
  matrix products  3.1 us (4%)
    all_gather x2, blocking collectives, timewise(): pieces = lax.all_gather(conserved_vars[None], 'inst', axis=0, tiled=True)  28.3 us
    ppermute x2, starting transfers between devices, extended(): lax.ppermute(tail, axis, [(i, (i + 1) % count) for i in range(ends)])  13 us
    ppermute x4, starting transfers between devices, from_behind(): return lax.ppermute(block, axis, route)  7.53 us
    ppermute x2, starting transfers between devices, extended(): lax.ppermute(head, axis, [((i + 1) % count, i) for i in range(ends)])  4.02 us
    dot_general x2, matrix products, timewise(): jnp.tensordot(weights, pieces, axes=1, precision=lax.Precision.HIGHEST)  3.1 us
    unnamed x24, other arithmetic  3.02 us
  transfers between devices with their start and end apart: 8, of which 0 were waited for; matrix products, arithmetic and copies ran while one was open for 16% of the time, Pallas kernels for 0%

commit v1 on v0

--- a/solution.py
+++ b/solution.py
@@ -9,6 +9,20 @@
 viscosity = 0.1
 pseudo_step = 0.03
 entropy_share = 0.1
+
+
+def _fix_series(packet):
+    high = jax.lax.axis_size("inst")
+    upper = jax.lax.axis_index("inst")
+    b_next, earlier = (high, upper)
+    wide_out, big = (packet, 1)
+    while big < b_next:
+        everything = jax.lax.ppermute(wide_out, "inst", [(q, q ^ big) for q in range(b_next)])
+        v_next = jnp.concatenate([wide_out, everything], 0)
+        z2 = jnp.concatenate([everything, wide_out], 0)
+        wide_out = jnp.where(earlier & big == 0, v_next, z2)
+        big = 2 * big
+    return wide_out
 
 
 def from_behind(block, axis, distance):
@@ -180,7 +194,7 @@
         return from_behind(plane, "inst", steps)
 
     def timewise(conserved_vars):
-        pieces = lax.all_gather(conserved_vars[None], "inst", axis=0, tiled=True)
+        pieces = _fix_series(conserved_vars[None])
         number = pieces.shape[0]
         others = jnp.arange(number, dtype=jnp.int32)
         weights = spectral_entry(instance - others, instances)

time: 72.7 us -> 71.8 us (0.988)
  blocking collectives: 28.3 us -> 0 us
  waiting for transfers between devices: 0.02 us -> 28 us
  starting transfers between devices: 24.6 us -> 23.3 us
    all_gather x2 -> x0, blocking collectives: 28.3 us -> none  [timewise(): pieces = lax.all_gather(conserved_vars[None], 'inst', axis=0, tiled=True)]
    ppermute x0 -> x4, waiting for transfers between devices: none -> 28 us  [_fix_series(): jax.lax.ppermute(wide_out, 'inst', [(q, q ^ big) for q in range(b_next)])]
    ppermute x2, starting transfers between devices: 13 us -> 9.36 us  [extended(): lax.ppermute(tail, axis, [(i, (i + 1) % count) for i in range(ends)])]
    ppermute x0 -> x4, starting transfers between devices: none -> 3.26 us  [_fix_series(): jax.lax.ppermute(wide_out, 'inst', [(q, q ^ big) for q in range(b_next)])]
    ppermute x4, starting transfers between devices: 7.53 us -> 6.63 us  [from_behind(): return lax.ppermute(block, axis, route)]
  transfers between devices with their start and end apart: 8 -> 12, of which waited for: 0 -> 2; matrix products, arithmetic and copies ran while one was open for 16% -> 17% of each run, Pallas kernels for 0% -> 0%
where the time goes in v1:
time: 71.8 us; the launch traced here: 71.1 us
  waiting for transfers between devices  28 us (39%)
  starting transfers between devices  23.3 us (32%)
  local copies, waits for them, and re-layouts  8.13 us (11%)
  other arithmetic  7.95 us (11%)
  matrix products  3.1 us (4%)
    ppermute x4, waiting for transfers between devices, _fix_series(): jax.lax.ppermute(wide_out, 'inst', [(q, q ^ big) for q in range(b_next)])  28 us
    ppermute x2, starting transfers between devices, extended(): lax.ppermute(tail, axis, [(i, (i + 1) % count) for i in range(ends)])  9.36 us
    ppermute x4, starting transfers between devices, from_behind(): return lax.ppermute(block, axis, route)  6.63 us
    ppermute x2, starting transfers between devices, extended(): lax.ppermute(head, axis, [((i + 1) % count, i) for i in range(ends)])  4.02 us
    ppermute x4, starting transfers between devices, _fix_series(): jax.lax.ppermute(wide_out, 'inst', [(q, q ^ big) for q in range(b_next)])  3.26 us
    dot_general x2, matrix products, timewise(): jnp.tensordot(weights, pieces, axes=1, precision=lax.Precision.HIGHEST)  3.1 us
    unnamed x24, other arithmetic  3.01 us
  transfers between devices with their start and end apart: 12, of which 2 were waited for; matrix products, arithmetic and copies ran while one was open for 17% of the time, Pallas kernels for 0%

profile of v1, /device:TPU:1, one launch (start us, length us, event | category | flops | bytes accessed | tf_op | source)
XLA Modules:
  0.0 71.1 jit_solution(3973791252100116838)
XLA Ops:
  0.0 0.7 copy-done.1
  0.7 1.0 %fusion.15 = f32[5,4,16,128]{3,2,1,0:T(8,128)S(1)} fusion(f32[1,5,4,16,128]{4,3,2,1,0:T(8,128)} %param.7, f32[5]{0:T(128)S(1)} %copy-done.1, f32[5]{0:T(128)S(1)} %copy-done.2), kind=kLoop, calls=%fused_computation.63 | loop fusion | flops 81920 | bytes 327720 | tf_op jit(solution)/shard_map/add | solution.py:55
  1.8 2.2 %collective-permute-start = (f32[1,5,4,16,128]{4,3,2,1,0:T(8,128)S(1)}, f32[1,5,4,16,128]{4,3,2,1,0:T(8,128)S(1)}, u32[]{:S(2)}, u32[]{:S(2)}) collective-permute-start(f32[1,5,4,16,128]{4,3,2,1,0:T(8,128)S(1)} %get-tuple-element.131), channel_id=1, source_target_pairs={{0,4},{4,0},{8,12},{12,8},{1,5},{5,1},{9,13},{13,9},{2,6},{6,2},{1... | collective-permute-start | bytes 491528 | tf_op jit(solution)/shard_map/ppermute | solution.py:20
  5.1 3.3 %collective-permute-start.5 = (f32[5,4,16]{0,1,2:T(4,128)S(1)}, f32[5,4,16]{0,1,2:T(4,128)S(1)}, u32[]{:S(2)}, u32[]{:S(2)}) collective-permute-start(f32[5,4,16]{0,1,2:T(4,128)S(1)} %bitcast.389), channel_id=1, source_target_pairs={{4,0},{8,4},{12,8},{0,12},{5,1},{9,5},{13,9},{1,13},{6,2},{10,6},{... | collective-permute-start | bytes 3848 | tf_op jit(solution)/shard_map/ppermute | solution.py:31
  8.4 4.5 %collective-permute-start.2 = (f32[5,1,16,128]{3,2,1,0:T(8,128)S(1)}, f32[5,1,16,128]{3,2,1,0:T(8,128)S(1)}, u32[]{:S(2)}, u32[]{:S(2)}) collective-permute-start(f32[5,1,16,128]{3,2,1,0:T(8,128)S(1)} %get-tuple-element.119), channel_id=1, source_target_pairs={{0,1},{1,2},{2,3},{4,5},{5,6},{6,7},{8,9},{9,10},{10,11},{12,13},{... | collective-permute-start | bytes 122888 | tf_op jit(solution)/shard_map/ppermute | solution.py:42
  12.9 1.9 %collective-permute-start.3 = (f32[5,1,16,128]{3,2,1,0:T(8,128)S(1)}, f32[5,1,16,128]{3,2,1,0:T(8,128)S(1)}, u32[]{:S(2)}, u32[]{:S(2)}) collective-permute-start(f32[5,1,16,128]{3,2,1,0:T(8,128)S(1)} %get-tuple-element.120), channel_id=1, source_target_pairs={{1,0},{2,1},{3,2},{5,4},{6,5},{7,6},{9,8},{10,9},{11,10},{13,12},{... | collective-permute-start | bytes 122888 | tf_op jit(solution)/shard_map/ppermute | solution.py:44
  15.0 0.6 copy-done
  16.6 0.6 gather_fusion
  17.3 0.6 copy.20
  17.8 0.6 gather_fusion.1
  18.5 0.6 copy.23
  20.8 0.6 collective-permute-start.1
  21.6 13.7 %collective-permute-done.1 = f32[2,5,4,16,128]{4,3,2,1,0:T(8,128)S(1)} collective-permute-done((f32[2,5,4,16,128]{4,3,2,1,0:T(8,128)S(1)}, f32[2,5,4,16,128]{4,3,2,1,0:T(8,128)S(1)}, u32[]{:S(2)}, u32[]{:S(2)}) %collective-permute-start.1) | collective-permute-done | bytes 327712 | tf_op jit(solution)/shard_map/ppermute | solution.py:20
  35.4 1.5 %fusion.2 = f32[1,5,4,16,128]{4,0,3,2,1:T(1,128)S(1)} fusion(f32[4,5,4,16,128]{4,3,2,1,0:T(8,128)S(1)} %maximum_select_fusion, s32[]{:T(128)S(6)} %axis_index.15), kind=kOutput, calls=%fused_computation.8 | convolution fusion | flops 1966224 | bytes 819204 | tf_op jit(solution)/shard_map/dot_general | solution.py:201
  38.0 1.5 %collective-permute-start.10 = (f32[5,4,16]{0,1,2:T(4,128)S(1)}, f32[5,4,16]{0,1,2:T(4,128)S(1)}, u32[]{:S(2)}, u32[]{:S(2)}) collective-permute-start(f32[5,4,16]{0,1,2:T(4,128)S(1)} %bitcast.392), channel_id=1, source_target_pairs={{12,0},{0,4},{4,8},{8,12},{13,1},{1,5},{5,9},{9,13},{14,2},{2,6},{... | collective-permute-start | bytes 3848 | tf_op jit(solution)/shard_map/ppermute | solution.py:31
  39.9 1.8 %collective-permute-start.11 = (f32[5,4,16]{0,1,2:T(4,128)S(1)}, f32[5,4,16]{0,1,2:T(4,128)S(1)}, u32[]{:S(2)}, u32[]{:S(2)}) collective-permute-start(f32[5,4,16]{0,1,2:T(4,128)S(1)} %bitcast.391), channel_id=1, source_target_pairs={{4,0},{8,4},{12,8},{0,12},{5,1},{9,5},{13,9},{1,13},{6,2},{10,6},{... | collective-permute-start | bytes 3848 | tf_op jit(solution)/shard_map/ppermute | solution.py:31
  42.4 4.8 %collective-permute-start.8 = (f32[5,1,16,128]{3,2,1,0:T(8,128)S(1)}, f32[5,1,16,128]{3,2,1,0:T(8,128)S(1)}, u32[]{:S(2)}, u32[]{:S(2)}) collective-permute-start(f32[5,1,16,128]{3,2,1,0:T(8,128)S(1)} %get-tuple-element.105), channel_id=1, source_target_pairs={{0,1},{1,2},{2,3},{4,5},{5,6},{6,7},{8,9},{9,10},{10,11},{12,13},{... | collective-permute-start | bytes 122888 | tf_op jit(solution)/shard_map/ppermute | solution.py:42
  47.3 2.1 %collective-permute-start.9 = (f32[5,1,16,128]{3,2,1,0:T(8,128)S(1)}, f32[5,1,16,128]{3,2,1,0:T(8,128)S(1)}, u32[]{:S(2)}, u32[]{:S(2)}) collective-permute-start(f32[5,1,16,128]{3,2,1,0:T(8,128)S(1)} %get-tuple-element.106), channel_id=1, source_target_pairs={{1,0},{2,1},{3,2},{5,4},{6,5},{7,6},{9,8},{10,9},{11,10},{13,12},{... | collective-permute-start | bytes 122888 | tf_op jit(solution)/shard_map/ppermute | solution.py:44
  49.5 0.6 gather_fusion.2
  50.2 0.6 copy.25
  50.8 0.6 gather_fusion.3
  54.4 14.2 %collective-permute-done.7 = f32[2,5,4,16,128]{4,3,2,1,0:T(8,128)S(1)} collective-permute-done((f32[2,5,4,16,128]{4,3,2,1,0:T(8,128)S(1)}, f32[2,5,4,16,128]{4,3,2,1,0:T(8,128)S(1)}, u32[]{:S(2)}, u32[]{:S(2)}) %collective-permute-start.7) | collective-permute-done | bytes 327712 | tf_op jit(solution)/shard_map/ppermute | solution.py:20
  68.7 1.5 %fusion = f32[1,5,4,16,128]{4,0,3,2,1:T(1,128)S(1)} fusion(f32[4,5,4,16,128]{4,3,2,1,0:T(8,128)S(1)} %maximum_select_fusion.1, s32[]{:T(128)S(6)} %axis_index.15), kind=kOutput, calls=%fused_computation.6 | convolution fusion | flops 1966224 | bytes 819204 | tf_op jit(solution)/shard_map/dot_general | solution.py:201
  70.3 0.8 %fusion.8 = f32[1,5,4,16,128]{4,3,2,1,0:T(8,128)} fusion(f32[5,4,16,128]{3,2,1,0:T(8,128)S(1)} %bitcast.387, f32[5,4,16,129]{3,2,1,0:T(8,128)S(1)} %fusion.51, f32[5,4,17,128]{3,2,1,0:T(8,128)S(1)} %constant_dynamic-update-slice_fusion.15, f32[5,5,16,128]{3,2,1,0:T(8,128)S(1)} %constant_dynamic-update-slice_fusion.10), kind=kLoop, calls=%fused_computation.49 | loop fusion | flops 245760 | bytes 1310720 | tf_op jit(solution)/shard_map/broadcast_in_dim | solution.py:226
  (104 shorter events, 9.5 us)
Async XLA Ops:
  0.0 0.7 copy-start.1
  0.0 0.7 copy-start.2
  1.8 19.0 %collective-permute-start = (f32[1,5,4,16,128]{4,3,2,1,0:T(8,128)S(1)}, f32[1,5,4,16,128]{4,3,2,1,0:T(8,128)S(1)}, u32[]{:S(2)}, u32[]{:S(2)}) collective-permute-start(f32[1,5,4,16,128]{4,3,2,1,0:T(8,128)S(1)} %get-tuple-element.131), channel_id=1, source_target_pairs={{0,4},{4,0},{8,12},{12,8},{1,5},{5,1},{9,13},{13,9},{2,6},{6,2},{1... | collective-permute-start | bytes 491528 | tf_op jit(solution)/shard_map/ppermute | solution.py:20
  4.6 12.0 %collective-permute-start.4 = (f32[5,4,16]{0,1,2:T(4,128)S(1)}, f32[5,4,16]{0,1,2:T(4,128)S(1)}, u32[]{:S(2)}, u32[]{:S(2)}) collective-permute-start(f32[5,4,16]{0,1,2:T(4,128)S(1)} %bitcast.390), channel_id=1, source_target_pairs={{12,0},{0,4},{4,8},{8,12},{13,1},{1,5},{5,9},{9,13},{14,2},{2,6},{... | collective-permute-start | bytes 3848 | tf_op jit(solution)/shard_map/ppermute | solution.py:31
  5.1 12.7 %collective-permute-start.5 = (f32[5,4,16]{0,1,2:T(4,128)S(1)}, f32[5,4,16]{0,1,2:T(4,128)S(1)}, u32[]{:S(2)}, u32[]{:S(2)}) collective-permute-start(f32[5,4,16]{0,1,2:T(4,128)S(1)} %bitcast.389), channel_id=1, source_target_pairs={{4,0},{8,4},{12,8},{0,12},{5,1},{9,5},{13,9},{1,13},{6,2},{10,6},{... | collective-permute-start | bytes 3848 | tf_op jit(solution)/shard_map/ppermute | solution.py:31
  8.4 6.5 %copy-start.3 = (s32[16]{0:T(128)S(1)}, s32[16]{0:T(128)}, u32[]{:S(2)}) copy-start(s32[16]{0:T(128)} %param.8) | copy-start | bytes 196
  8.4 11.9 %collective-permute-start.2 = (f32[5,1,16,128]{3,2,1,0:T(8,128)S(1)}, f32[5,1,16,128]{3,2,1,0:T(8,128)S(1)}, u32[]{:S(2)}, u32[]{:S(2)}) collective-permute-start(f32[5,1,16,128]{3,2,1,0:T(8,128)S(1)} %get-tuple-element.119), channel_id=1, source_target_pairs={{0,1},{1,2},{2,3},{4,5},{5,6},{6,7},{8,9},{9,10},{10,11},{12,13},{... | collective-permute-start | bytes 122888 | tf_op jit(solution)/shard_map/ppermute | solution.py:42
  12.9 7.3 %collective-permute-start.3 = (f32[5,1,16,128]{3,2,1,0:T(8,128)S(1)}, f32[5,1,16,128]{3,2,1,0:T(8,128)S(1)}, u32[]{:S(2)}, u32[]{:S(2)}) collective-permute-start(f32[5,1,16,128]{3,2,1,0:T(8,128)S(1)} %get-tuple-element.120), channel_id=1, source_target_pairs={{1,0},{2,1},{3,2},{5,4},{6,5},{7,6},{9,8},{10,9},{11,10},{13,12},{... | collective-permute-start | bytes 122888 | tf_op jit(solution)/shard_map/ppermute | solution.py:44
  15.0 0.7 copy-start
  20.8 14.5 %collective-permute-start.1 = (f32[2,5,4,16,128]{4,3,2,1,0:T(8,128)S(1)}, f32[2,5,4,16,128]{4,3,2,1,0:T(8,128)S(1)}, u32[]{:S(2)}, u32[]{:S(2)}) collective-permute-start(f32[2,5,4,16,128]{4,3,2,1,0:T(8,128)S(1)} %maximum_select_fusion.2), channel_id=1, source_target_pairs={{0,8},{4,12},{8,0},{12,4},{1,9},{5,13},{9,1},{13,5},{2,10},{6,14},... | collective-permute-start | bytes 983048 | tf_op jit(solution)/shard_map/ppermute | solution.py:20
  37.4 16.4 %collective-permute-start.6 = (f32[1,5,4,16,128]{4,3,2,1,0:T(8,128)S(1)}, f32[1,5,4,16,128]{4,3,2,1,0:T(8,128)S(1)}, u32[]{:S(2)}, u32[]{:S(2)}) collective-permute-start(f32[1,5,4,16,128]{4,3,2,1,0:T(8,128)S(1)} %bitcast.385), channel_id=1, source_target_pairs={{0,4},{4,0},{8,12},{12,8},{1,5},{5,1},{9,13},{13,9},{2,6},{6,2},{1... | collective-permute-start | bytes 491528 | tf_op jit(solution)/shard_map/ppermute | solution.py:20
  38.0 11.6 %collective-permute-start.10 = (f32[5,4,16]{0,1,2:T(4,128)S(1)}, f32[5,4,16]{0,1,2:T(4,128)S(1)}, u32[]{:S(2)}, u32[]{:S(2)}) collective-permute-start(f32[5,4,16]{0,1,2:T(4,128)S(1)} %bitcast.392), channel_id=1, source_target_pairs={{12,0},{0,4},{4,8},{8,12},{13,1},{1,5},{5,9},{9,13},{14,2},{2,6},{... | collective-permute-start | bytes 3848 | tf_op jit(solution)/shard_map/ppermute | solution.py:31
  39.9 10.9 %collective-permute-start.11 = (f32[5,4,16]{0,1,2:T(4,128)S(1)}, f32[5,4,16]{0,1,2:T(4,128)S(1)}, u32[]{:S(2)}, u32[]{:S(2)}) collective-permute-start(f32[5,4,16]{0,1,2:T(4,128)S(1)} %bitcast.391), channel_id=1, source_target_pairs={{4,0},{8,4},{12,8},{0,12},{5,1},{9,5},{13,9},{1,13},{6,2},{10,6},{... | collective-permute-start | bytes 3848 | tf_op jit(solution)/shard_map/ppermute | solution.py:31
  42.4 10.8 %collective-permute-start.8 = (f32[5,1,16,128]{3,2,1,0:T(8,128)S(1)}, f32[5,1,16,128]{3,2,1,0:T(8,128)S(1)}, u32[]{:S(2)}, u32[]{:S(2)}) collective-permute-start(f32[5,1,16,128]{3,2,1,0:T(8,128)S(1)} %get-tuple-element.105), channel_id=1, source_target_pairs={{0,1},{1,2},{2,3},{4,5},{5,6},{6,7},{8,9},{9,10},{10,11},{12,13},{... | collective-permute-start | bytes 122888 | tf_op jit(solution)/shard_map/ppermute | solution.py:42
  47.3 6.0 %collective-permute-start.9 = (f32[5,1,16,128]{3,2,1,0:T(8,128)S(1)}, f32[5,1,16,128]{3,2,1,0:T(8,128)S(1)}, u32[]{:S(2)}, u32[]{:S(2)}) collective-permute-start(f32[5,1,16,128]{3,2,1,0:T(8,128)S(1)} %get-tuple-element.106), channel_id=1, source_target_pairs={{1,0},{2,1},{3,2},{5,4},{6,5},{7,6},{9,8},{10,9},{11,10},{13,12},{... | collective-permute-start | bytes 122888 | tf_op jit(solution)/shard_map/ppermute | solution.py:44
  53.8 14.9 %collective-permute-start.7 = (f32[2,5,4,16,128]{4,3,2,1,0:T(8,128)S(1)}, f32[2,5,4,16,128]{4,3,2,1,0:T(8,128)S(1)}, u32[]{:S(2)}, u32[]{:S(2)}) collective-permute-start(f32[2,5,4,16,128]{4,3,2,1,0:T(8,128)S(1)} %maximum_select_fusion.3), channel_id=1, source_target_pairs={{0,8},{4,12},{8,0},{12,4},{1,9},{5,13},{9,1},{13,5},{2,10},{6,14},... | collective-permute-start | bytes 983048 | tf_op jit(solution)/shard_map/ppermute | solution.py:20
